TPU v7x, 32 devices: a whole 2x2x4 slice. The times are simulated.
32 devices in a mesh: nodes: 8 (over z, y), mp: 4 (over x, core).
Axes of the slice: x: 2, y: 2, z: 4, core: 2. Of those that a mesh axis runs over, the one named last changes fastest.
Arguments:
- query: bfloat16 [2048, 512], P('nodes', 'mp'), may hold values from -240 to 240
- key: bfloat16 [2048, 512], P('nodes', 'mp'), may hold values from -7 to 7
- value: bfloat16 [2048, 512], P('nodes', 'mp'), may hold values from -12 to 12
- out_weight: bfloat16 [512, 512], P('mp'), may hold values from -0.25 to 0.25
- cotangent: bfloat16 [2048, 512], P('nodes', 'mp'), may hold values from -6 to 6
- virtual_key: bfloat16 [64, 512], P('nodes', 'mp'), may hold values from -6 to 6
- virtual_value: bfloat16 [64, 512], P('nodes', 'mp'), may hold values from -12 to 12
- halo_rows: int32 [8, 2, 128], P('nodes'), may hold values from 0 to 255
- halo_live: int32 [8, 2], P('nodes'), may hold values from 64 to 128, as said below
- expand_rows: int32 [8, 8, 2], P('nodes'), may hold values from 0 to 255
- local_mask: int32 [16, 4], P('nodes'), may hold values from 0 to 1, as said below
- expand_mask: int32 [16, 8], P('nodes'), may hold values 0 or 1
Outputs:
- output: bfloat16 [2048, 512], P('nodes', 'mp')
- grad_query: float32 [2048, 512], P('nodes', 'mp')
- grad_key: float32 [2048, 512], P('nodes', 'mp')
- grad_value: float32 [2048, 512], P('nodes', 'mp')
- grad_virtual_key: float32 [64, 512], P('nodes', 'mp')
- grad_virtual_value: float32 [64, 512], P('nodes', 'mp')
Inputs may be any that keep to these rules, and one draw needn't show every extreme that they name: halo_rows[p, 0, :] index nodes of partition p (0 to 255) sent to partition p + 1, halo_rows[p, 1, :] those sent to partition p - 1; repeats possible. Only the leading halo_live slots of what a partition receives from a neighbour are edges; the value 128 occurs in every draw. expand_rows[r, p, :] index nodes of partition r. Every query tile attends its own tile and both received boundary tiles: local_mask[t, t mod 2], local_mask[t, 2] and local_mask[t, 3] are 1.
All inputs are finite; a program needn't handle non-finite values. No bound on the sum of `expand_mask` on one device may be relied on, other than what follows from the above.
Results may differ from a plain program's by a relative error of at most 0.034.
Values may be sent and summed in bfloat16 or wider, within the bound.
A program may use at most 64 MiB of HBM per device.

v0:
```python
import jax
import jax.numpy as jnp
from jax import lax
from jax.sharding import PartitionSpec as P

HEADS = 8


def extended(array, sides, width):
    for axis, dim in sides:
        devices, length = (lax.axis_size(axis), array.shape[dim])
        up = [(i, (i + 1) % devices) for i in range(devices)]
        down = [(j, i) for i, j in up]
        last = lax.slice_in_dim(array, length - width, length, axis=dim)
        leading = lax.slice_in_dim(array, 0, width, axis=dim)
        before = lax.ppermute(last, axis, up)
        after = lax.ppermute(leading, axis, down)
        array = jnp.concatenate([before, array, after], axis=dim)
    return array


def edge_mask(local_block, expand_block, live, tile_rows, halo_cap, exp_slot, virtual_count):
    tile_count = local_block.shape[0]
    own_tiles = jnp.repeat(
        jnp.repeat(local_block[:, :tile_count] > 0, tile_rows, axis=0), tile_rows, axis=1
    )
    slot_index = jnp.arange(halo_cap)
    left_ok = (local_block[:, tile_count] > 0)[:, None] & (slot_index < live[0])[None, :]
    right_ok = (local_block[:, tile_count + 1] > 0)[:, None] & (slot_index < live[1])[None, :]
    expand_ok = jnp.repeat(expand_block > 0, exp_slot, axis=1)
    remote_tiles = jnp.repeat(
        jnp.concatenate([left_ok, right_ok, expand_ok], axis=1), tile_rows, axis=0
    )
    virtual_ok = jnp.ones((tile_count * tile_rows, virtual_count), dtype=jnp.bool_)
    return jnp.concatenate([own_tiles, remote_tiles, virtual_ok], axis=1)


def body(
    query,
    key,
    value,
    out_weight,
    cotangent,
    virtual_key,
    virtual_value,
    halo_rows,
    halo_live,
    expand_rows,
    local_mask,
    expand_mask,
):
    node_rows, width = query.shape
    heads_dev = HEADS // lax.axis_size("mp")
    head_dim = width // heads_dev
    score_scale = head_dim ** (-0.5)
    tile_count = local_mask.shape[0]
    tile_rows = node_rows // tile_count
    halo_cap = halo_rows.shape[2]
    peer_count = expand_rows.shape[1]
    exp_slot = expand_rows.shape[2]
    to_right = halo_rows[0, 0]
    to_left = halo_rows[0, 1]
    expand_flat = expand_rows[0].reshape(-1)
    key_value = jnp.concatenate([key, value], axis=1)
    outgoing_rows = jnp.concatenate([key_value[to_left], key_value[to_right]], axis=0)
    padded = extended(outgoing_rows, (("nodes", 0),), halo_cap)
    from_left = padded[:halo_cap]
    from_right = padded[3 * halo_cap :]
    expand_sent = key_value[expand_flat].reshape(peer_count, exp_slot, 2 * width)
    arrived = lax.all_to_all(expand_sent, "nodes", split_axis=0, concat_axis=0, tiled=True).reshape(
        peer_count * exp_slot, 2 * width
    )
    all_virtual_key, all_virtual_value = (
        lax.all_gather(virtual_key, "nodes", axis=0, tiled=True),
        lax.all_gather(virtual_value, "nodes", axis=0, tiled=True),
    )
    virtual_count = all_virtual_key.shape[0]
    all_keys = jnp.concatenate(
        [key, from_left[:, :width], from_right[:, :width], arrived[:, :width], all_virtual_key],
        axis=0,
    )
    all_values = jnp.concatenate(
        [value, from_left[:, width:], from_right[:, width:], arrived[:, width:], all_virtual_value],
        axis=0,
    )
    allowed = edge_mask(
        local_mask, expand_mask, halo_live[0], tile_rows, halo_cap, exp_slot, virtual_count
    )
    d_attn = jnp.einsum(
        "nc,wc->nw",
        lax.all_gather(cotangent, "mp", axis=1, tiled=True),
        out_weight,
        preferred_element_type=jnp.float32,
    ).astype(jnp.bfloat16)
    attn_parts = []
    grad_query_parts = []
    grad_key_parts = []
    grad_value_parts = []
    for head_number in range(heads_dev):
        low = head_number * head_dim
        high = low + head_dim
        query_head = query[:, low:high]
        key_head = all_keys[:, low:high]
        value_head = all_values[:, low:high]
        grad_head = d_attn[:, low:high]
        scores = (
            jnp.einsum("qd,kd->qk", query_head, key_head, preferred_element_type=jnp.float32)
            * score_scale
        )
        scores = jnp.where(allowed, scores, -1e30)
        row_max = jnp.max(scores, axis=1, keepdims=True)
        weights = jnp.exp(scores - row_max)
        probs = weights / jnp.sum(weights, axis=1, keepdims=True)
        probs_b = probs.astype(jnp.bfloat16)
        attn_head = jnp.dot(probs_b, value_head, preferred_element_type=jnp.float32).astype(
            jnp.bfloat16
        )
        d_prob = jnp.einsum("qd,kd->qk", grad_head, value_head, preferred_element_type=jnp.float32)
        row_delta = jnp.sum(
            grad_head.astype(jnp.float32) * attn_head.astype(jnp.float32), axis=1, keepdims=True
        )
        d_score = (probs * (d_prob - row_delta) * score_scale).astype(jnp.bfloat16)
        attn_parts.append(attn_head)
        grad_query_parts.append(jnp.dot(d_score, key_head, preferred_element_type=jnp.float32))
        grad_key_parts.append(
            jnp.einsum("qk,qd->kd", d_score, query_head, preferred_element_type=jnp.float32)
        )
        grad_value_parts.append(
            jnp.einsum("qk,qd->kd", probs_b, grad_head, preferred_element_type=jnp.float32)
        )
    attn = jnp.concatenate(attn_parts, axis=1)
    grad_query = jnp.concatenate(grad_query_parts, axis=1)
    grad_keys = jnp.concatenate(grad_key_parts, axis=1)
    grad_values = jnp.concatenate(grad_value_parts, axis=1)
    projected = jnp.dot(attn, out_weight, preferred_element_type=jnp.float32)
    output = lax.psum_scatter(projected, "mp", scatter_dimension=1, tiled=True).astype(jnp.bfloat16)
    left_end = node_rows + halo_cap
    right_end = left_end + halo_cap
    expand_end = right_end + peer_count * exp_slot
    grad_pairs = jnp.concatenate([grad_keys, grad_values], axis=1)
    halo_back = grad_pairs[node_rows:right_end]
    returned = extended(halo_back, (("nodes", 0),), halo_cap)
    for_left_sent = returned[:halo_cap]
    for_right_sent = returned[3 * halo_cap :]
    expand_back = grad_pairs[right_end:expand_end].reshape(peer_count, exp_slot, 2 * width)
    came_home = lax.all_to_all(
        expand_back, "nodes", split_axis=0, concat_axis=0, tiled=True
    ).reshape(peer_count * exp_slot, 2 * width)
    own_grads = grad_pairs[:node_rows]
    own_grads = own_grads.at[to_left].add(for_left_sent)
    own_grads = own_grads.at[to_right].add(for_right_sent)
    own_grads = own_grads.at[expand_flat].add(came_home)
    grad_key = own_grads[:, :width]
    grad_value = own_grads[:, width:]
    virtual_key_term = grad_keys[expand_end:]
    virtual_value_term = grad_values[expand_end:]
    grad_virtual_key, grad_virtual_value = (
        lax.psum_scatter(virtual_key_term, "nodes", scatter_dimension=0, tiled=True),
        lax.psum_scatter(virtual_value_term, "nodes", scatter_dimension=0, tiled=True),
    )
    return (output, grad_query, grad_key, grad_value, grad_virtual_key, grad_virtual_value)


def solution(mesh):
    return jax.shard_map(
        body,
        mesh=mesh,
        in_specs=(
            P("nodes", "mp"),
            P("nodes", "mp"),
            P("nodes", "mp"),
            P("mp", None),
            P("nodes", "mp"),
            P("nodes", "mp"),
            P("nodes", "mp"),
            P("nodes", None, None),
            P("nodes", None),
            P("nodes", None, None),
            P("nodes", None),
            P("nodes", None),
        ),
        out_specs=(
            P("nodes", "mp"),
            P("nodes", "mp"),
            P("nodes", "mp"),
            P("nodes", "mp"),
            P("nodes", "mp"),
            P("nodes", "mp"),
        ),
        check_vma=False,
    )
```

profile of v0, /device:TPU:0, one launch (start us, length us, event | category | flops | bytes accessed | tf_op | source)
XLA Modules:
  0.0 192.0 jit_solution(5253378758399897791)
XLA Ops:
  8.0 0.8 copy.38
  8.9 0.9 constant_dynamic-update-slice_fusion.1
  9.8 0.6 gather_fusion.2
  10.4 0.6 reshape.142
  11.0 7.4 %all-to-all-start = ((bf16[8,2,256]{2,1,0:T(2,128)(2,1)}), bf16[8,2,256]{2,1,0:T(2,128)(2,1)S(1)}, u32[]{:S(2)}, u32[]{:S(2)}) async-start(bf16[8,2,256]{2,1,0:T(2,128)(2,1)} %reshape.142), calls=%async_computation | async-start | bytes 16384 | tf_op jit(solution)/shard_map/all_to_all | solution.py:70
  18.5 0.8 gather_fusion
  19.3 2.1 %collective-permute-start = (bf16[128,256]{1,0:T(8,128)(2,1)S(1)}, bf16[128,256]{1,0:T(8,128)(2,1)S(1)}, u32[]{:S(2)}, u32[]{:S(2)}) collective-permute-start(bf16[128,256]{1,0:T(8,128)(2,1)S(1)} %gather_fusion), channel_id=1, source_target_pairs={{0,4},{4,8},{8,12},{12,16},{16,20},{20,24},{24,28},{28,0},{1,5},{5... | collective-permute-start | bytes 196616 | tf_op jit(solution)/shard_map/ppermute | solution.py:16
  21.4 0.8 gather_fusion.1
  22.3 2.8 %collective-permute-start.1 = (bf16[128,256]{1,0:T(8,128)(2,1)S(1)}, bf16[128,256]{1,0:T(8,128)(2,1)S(1)}, u32[]{:S(2)}, u32[]{:S(2)}) collective-permute-start(bf16[128,256]{1,0:T(8,128)(2,1)S(1)} %gather_fusion.1), channel_id=1, source_target_pairs={{4,0},{8,4},{12,8},{16,12},{20,16},{24,20},{28,24},{0,28},{5,1},{9... | collective-permute-start | bytes 196616 | tf_op jit(solution)/shard_map/ppermute | solution.py:17
  27.1 0.6 iota_compare_fusion.1
  27.8 0.7 iota_compare_fusion
  28.6 5.8 %all_gather.11 = bf16[256,512]{1,0:T(8,128)(2,1)S(1)} all-gather(bf16[256,128]{1,0:T(8,128)(2,1)S(1)} %copy-done.3), channel_id=1, replica_groups=mesh['nodes'=8,'mp'=4] {'mp'}, dimensions={1}, use_global_device_ids=true | all-gather | bytes 327680 | tf_op jit(solution)/shard_map/all_gather | solution.py:91
  35.0 0.6 copy-done.11
  37.5 26.1 %all_gather.9 = bf16[64,128]{1,0:T(8,128)(2,1)S(1)} all-gather(bf16[8,128]{1,0:T(8,128)(2,1)S(1)} %copy-done.6), channel_id=1, replica_groups=mesh['nodes'=8,'mp'=4] {'nodes'}, dimensions={0}, use_global_device_ids=true | all-gather | bytes 18432 | tf_op jit(solution)/shard_map/all_gather | solution.py:74
  63.7 26.0 %all_gather.10 = bf16[64,128]{1,0:T(8,128)(2,1)S(1)} all-gather(bf16[8,128]{1,0:T(8,128)(2,1)S(1)} %copy-done.7), channel_id=1, replica_groups=mesh['nodes'=8,'mp'=4] {'nodes'}, dimensions={0}, use_global_device_ids=true | all-gather | bytes 18432 | tf_op jit(solution)/shard_map/all_gather | solution.py:75
  89.8 0.8 copy-done.1
  93.8 0.7 pad_maximum_fusion.6
  94.6 0.7 pad_maximum_fusion.5
  95.4 0.6 reshape.144
  96.0 3.3 %all-to-all-start.1 = ((f32[8,2,256]{2,1,0:T(2,128)}), f32[8,2,256]{2,1,0:T(2,128)S(1)}, u32[]{:S(2)}, u32[]{:S(2)}) async-start(f32[8,2,256]{2,1,0:T(2,128)} %reshape.144), calls=%async_computation.2 | async-start | bytes 32768 | tf_op jit(solution)/shard_map/all_to_all | solution.py:146
  99.4 1.0 fusion.26
  101.7 0.8 copy.43
  102.6 4.7 %collective-permute-start.3 = (f32[128,256]{0,1:T(8,128)S(1)}, f32[128,256]{0,1:T(8,128)S(1)}, u32[]{:S(2)}, u32[]{:S(2)}) collective-permute-start(f32[128,256]{0,1:T(8,128)S(1)} %get-tuple-element.30), channel_id=1, source_target_pairs={{4,0},{8,4},{12,8},{16,12},{20,16},{24,20},{28,24},{0,28},{5,1},{9... | collective-permute-start | bytes 393224 | tf_op jit(solution)/shard_map/ppermute | solution.py:17
  107.3 68.6 %all-reduce.5.cloned.1.call-done = (f32[64,128]{0,1:T(8,128)}, f32[64,128]{0,1:T(8,128)}) async-done(((f32[64,128]{0,1:T(8,128)}, f32[64,128]{0,1:T(8,128)}), (f32[64,128]{0,1:T(8,128)}, f32[64,128]{0,1:T(8,128)})) %all-reduce.5.cloned.1.call-update) | async-done | bytes 65552
  175.9 0.9 constant_dynamic-slice_fusion.1
  176.8 0.7 copy.44
  177.8 0.7 copy.45
  178.5 1.4 scatter_fusion
  180.1 1.4 scatter_fusion.1
  181.5 0.8 scatter_fusion.2
  182.3 0.7 fusion.46
  183.0 1.5 convert_element_type.40
  (92 shorter events, 9.4 us)
Async XLA Ops:
  8.0 26.4 %copy-start = (bf16[128,512]{1,0:T(8,128)(2,1)S(1)}, bf16[128,512]{1,0:T(8,128)(2,1)}, u32[]{:S(2)}) copy-start(bf16[128,512]{1,0:T(8,128)(2,1)} %param.15) | copy-start | bytes 393220
  8.9 0.9 copy-start.2
  11.0 7.4 %copy-start.9 = (s32[1,2,128]{2,1,0:T(2,128)S(1)}, s32[1,2,128]{2,1,0:T(2,128)}, u32[]{:S(2)}) copy-start(s32[1,2,128]{2,1,0:T(2,128)} %param.19) | copy-start | bytes 3076
  11.0 78.6 %all-to-all-start = ((bf16[8,2,256]{2,1,0:T(2,128)(2,1)}), bf16[8,2,256]{2,1,0:T(2,128)(2,1)S(1)}, u32[]{:S(2)}, u32[]{:S(2)}) async-start(bf16[8,2,256]{2,1,0:T(2,128)(2,1)} %reshape.142), calls=%async_computation | async-start | bytes 16384 | tf_op jit(solution)/shard_map/all_to_all | solution.py:70
  19.3 70.3 %collective-permute-start = (bf16[128,256]{1,0:T(8,128)(2,1)S(1)}, bf16[128,256]{1,0:T(8,128)(2,1)S(1)}, u32[]{:S(2)}, u32[]{:S(2)}) collective-permute-start(bf16[128,256]{1,0:T(8,128)(2,1)S(1)} %gather_fusion), channel_id=1, source_target_pairs={{0,4},{4,8},{8,12},{12,16},{16,20},{20,24},{24,28},{28,0},{1,5},{5... | collective-permute-start | bytes 196616 | tf_op jit(solution)/shard_map/ppermute | solution.py:16
  21.4 3.6 %copy-start.5 = (s32[2,4]{1,0:T(2,128)S(1)}, s32[2,4]{1,0:T(2,128)}, u32[]{:S(2)}) copy-start(s32[2,4]{1,0:T(2,128)} %param.22) | copy-start | bytes 100
  21.4 7.2 %copy-start.3 = (bf16[256,128]{1,0:T(8,128)(2,1)S(1)}, bf16[256,128]{1,0:T(8,128)(2,1)}, u32[]{:S(2)}) copy-start(bf16[256,128]{1,0:T(8,128)(2,1)} %param.16) | copy-start | bytes 196612
  22.3 67.4 %collective-permute-start.1 = (bf16[128,256]{1,0:T(8,128)(2,1)S(1)}, bf16[128,256]{1,0:T(8,128)(2,1)S(1)}, u32[]{:S(2)}, u32[]{:S(2)}) collective-permute-start(bf16[128,256]{1,0:T(8,128)(2,1)S(1)} %gather_fusion.1), channel_id=1, source_target_pairs={{4,0},{8,4},{12,8},{16,12},{20,16},{24,20},{28,24},{0,28},{5,1},{9... | collective-permute-start | bytes 196616 | tf_op jit(solution)/shard_map/ppermute | solution.py:17
  25.1 0.7 copy-start.10
  25.9 0.7 copy-start.8
  35.0 0.7 copy-start.11
  36.9 0.7 copy-start.6
  37.5 26.1 %copy-start.7 = (bf16[8,128]{1,0:T(8,128)(2,1)S(1)}, bf16[8,128]{1,0:T(8,128)(2,1)}, u32[]{:S(2)}) copy-start(bf16[8,128]{1,0:T(8,128)(2,1)} %param.18) | copy-start | bytes 6148
  89.7 0.8 copy-start.1
  96.0 11.2 %all-to-all-start.1 = ((f32[8,2,256]{2,1,0:T(2,128)}), f32[8,2,256]{2,1,0:T(2,128)S(1)}, u32[]{:S(2)}, u32[]{:S(2)}) async-start(f32[8,2,256]{2,1,0:T(2,128)} %reshape.144), calls=%async_computation.2 | async-start | bytes 32768 | tf_op jit(solution)/shard_map/all_to_all | solution.py:146
  99.4 76.5 %all-reduce.5.cloned.1.call-start = ((), (), s32[]{:S(2)}) async-start(), calls=%async_computation.4 | async-start | bytes 262144
  100.5 82.5 %reduce-scatter.4.cloned.1.call-start = ((), (), s32[]{:S(2)}) async-start(), calls=%async_computation.3 | async-start | bytes 655360 | tf_op jit(solution)/shard_map/reduce_scatter | solution.py:136
  102.6 77.4 %collective-permute-start.3 = (f32[128,256]{0,1:T(8,128)S(1)}, f32[128,256]{0,1:T(8,128)S(1)}, u32[]{:S(2)}, u32[]{:S(2)}) collective-permute-start(f32[128,256]{0,1:T(8,128)S(1)} %get-tuple-element.30), channel_id=1, source_target_pairs={{4,0},{8,4},{12,8},{16,12},{20,16},{24,20},{28,24},{0,28},{5,1},{9... | collective-permute-start | bytes 393224 | tf_op jit(solution)/shard_map/ppermute | solution.py:17
  107.2 71.2 %collective-permute-start.2 = (f32[128,256]{0,1:T(8,128)S(1)}, f32[128,256]{0,1:T(8,128)S(1)}, u32[]{:S(2)}, u32[]{:S(2)}) collective-permute-start(f32[128,256]{0,1:T(8,128)S(1)} %get-tuple-element.31), channel_id=1, source_target_pairs={{0,4},{4,8},{8,12},{12,16},{16,20},{20,24},{24,28},{28,0},{1,5},{5... | collective-permute-start | bytes 393224 | tf_op jit(solution)/shard_map/ppermute | solution.py:16
  176.8 0.8 copy-start.4
Sparse Core Ops, SparseCore 0:
  104.7 71.2 all-reduce.4
Sparse Core Ops, SparseCore 1:
  103.5 22.9 reduce-scatter.3
where the time goes:
time: 193 us; the launch traced here: 192 us
  waiting for transfers between devices  69.2 us (36%)
  blocking collectives  57.9 us (30%)
  starting transfers between devices  20.4 us (11%)
  between operations  16.5 us (9%)
  local copies, waits for them, and re-layouts  14.7 us (8%)
  other arithmetic  8.82 us (5%)
  matrix products  4.52 us (2%)
    unnamed x3, waiting for transfers between devices  69.2 us
    all_gather x1, blocking collectives, body(): lax.all_gather(virtual_key, 'nodes', axis=0, tiled=True)  26.1 us
    all_gather x1, blocking collectives, body(): lax.all_gather(virtual_value, 'nodes', axis=0, tiled=True)  26 us
    unnamed x38, local copies, waits for them, and re-layouts  8.75 us
    ppermute x2, starting transfers between devices, extended(): after = lax.ppermute(leading, axis, down)  7.45 us
    all_to_all x1, starting transfers between devices, body(): lax.all_to_all(expand_sent, 'nodes', split_axis=0, concat_axis=0, tiled=T...  7.41 us
    all_gather x1, blocking collectives, body(): lax.all_gather(cotangent, 'mp', axis=1, tiled=True)  5.81 us
  transfers between devices with their start and end apart: 8, of which 1 were waited for; matrix products, arithmetic and copies ran while one was open for 8% of the time, Pallas kernels for 0%

commit v1 on v0

v1 whole, which is shorter than its diff:
```python
import functools

import jax
import jax.numpy as jnp
from jax import lax
from jax.experimental import pallas as pl
from jax.experimental.pallas import tpu as pltpu
from jax.sharding import PartitionSpec as P

HEADS = 8
MESH = pl.DeviceIdType.MESH
BF = jnp.bfloat16
F32 = jnp.float32
MASKED = -1e30

NN = (((1,), (0,)), ((), ()))
NT = (((1,), (1,)), ((), ()))
TN = (((0,), (0,)), ((), ()))


def mm(a, b, dims):
    return lax.dot_general(a, b, dims, preferred_element_type=F32)


def iota(shape, axis):
    return lax.broadcasted_iota(jnp.int32, shape, axis)


def each(count, step):
    if count <= 8:
        for d in range(count):
            step(d)
    else:
        pl.loop(0, count)(step)


def kernel(
    n, mp, heads,
    live, erows, lmask, emask,
    q_hbm, k_hbm, v_hbm, w_hbm, cot_hbm, vk_hbm, vv_hbm, hrows_hbm,
    out_hbm, gq_hbm, gk_hbm, gv_hbm, gvk_hbm, gvv_hbm,
    q_v, w_v, vk_v, vv_v, hrows, kv, cot, bias, onehot, mix_send, halo_send,
    e_ref, pb_ref, ds_ref, gback, ret_halo, ret_mix, proj, proj_in, own_v,
    out_v, gq_v, gk_v, gv_v, gvk_v, gvv_v,
    in_sem, out_sem, halo_s, halo_r, mix_s, mix_r, cot_s, cot_r, proj_s, proj_r,
    hb_s, hb_r, mb_s, mb_r,
):
    me = lax.axis_index("nodes")
    mm_i = lax.axis_index("mp")
    rows, width = q_v.shape
    tiles = lmask.shape[0]
    tile = rows // tiles
    cap = hrows.shape[2]
    slots = erows.shape[2]
    vn = vk_v.shape[0]
    blk = ret_mix.shape[0] // n
    hd = width // heads
    cols = heads * rows
    left, right = lax.rem(me + n - 1, n), lax.rem(me + 1, n)
    mix0 = rows + 2 * cap
    total = mix0 + n * blk

    barrier = pltpu.get_barrier_semaphore()

    def hello(d):
        pl.semaphore_signal(
            barrier, inc=1, device_id={"nodes": lax.rem(me + d + 1, n)}, device_id_type=MESH
        )

    each(n - 1, hello)
    for d in range(1, mp):
        pl.semaphore_signal(
            barrier, inc=1, device_id={"mp": lax.rem(mm_i + d, mp)}, device_id_type=MESH
        )

    loads = [
        pltpu.make_async_copy(k_hbm, kv.at[:rows, :width], in_sem.at[0]),
        pltpu.make_async_copy(v_hbm, kv.at[:rows, width:], in_sem.at[1]),
        pltpu.make_async_copy(hrows_hbm, hrows, in_sem.at[2]),
        pltpu.make_async_copy(vk_hbm, vk_v, in_sem.at[3]),
        pltpu.make_async_copy(vv_hbm, vv_v, in_sem.at[4]),
        pltpu.make_async_copy(cot_hbm, cot.at[mm_i], in_sem.at[5]),
        pltpu.make_async_copy(q_hbm, q_v, in_sem.at[6]),
        pltpu.make_async_copy(w_hbm, w_v, in_sem.at[7]),
    ]
    for c in loads:
        c.start()

    row_b, lane_b = iota((blk, rows), 0), iota((blk, rows), 1)

    def fill(d):
        peer = lax.rem(me + d, n)
        target = jnp.full((blk, rows), -1, jnp.int32)
        for s in range(slots):
            target = jnp.where(row_b == vn + s, erows[0, peer, s], target)
        onehot[pl.ds(d * blk, blk), :] = jnp.where(lane_b == target, 1.0, 0.0).astype(BF)

    each(n, fill)

    for c in loads[:5]:
        c.wait()
    own = kv[:rows, :]
    g_right = jnp.where(iota((rows, cap), 0) == hrows[0, 0:1, :], 1.0, 0.0).astype(BF)
    g_left = jnp.where(iota((rows, cap), 0) == hrows[0, 1:2, :], 1.0, 0.0).astype(BF)
    halo_send[0] = mm(g_right, own, TN).astype(BF)
    halo_send[1] = mm(g_left, own, TN).astype(BF)
    virt = jnp.concatenate([vk_v[...].astype(F32), vv_v[...].astype(F32)], axis=1)
    virt = jnp.concatenate([virt, jnp.zeros((blk - vn, 2 * width), F32)], axis=0)
    taken = mm(onehot[...], own, NN).reshape(n, blk, 2 * width) + virt[None]
    taken = taken.astype(BF)
    mix_send[...] = taken.reshape(n * blk, 2 * width)
    kv[mix0 : mix0 + blk, :] = taken[0]
    loads[5].wait()

    pl.semaphore_wait(barrier, n - 1 + mp - 1)

    def halo_copy(side):
        start = rows + side * cap
        return pltpu.make_async_remote_copy(
            halo_send.at[side], kv.at[start : start + cap, :], halo_s.at[side], halo_r.at[side],
            device_id={"nodes": right if side == 0 else left}, device_id_type=MESH,
        )

    def mix_copy(d):
        return pltpu.make_async_remote_copy(
            mix_send.at[pl.ds(d * blk, blk), :], kv.at[pl.ds(mix0 + d * blk, blk), :],
            mix_s.at[d], mix_r.at[d],
            device_id={"nodes": lax.rem(me + d, n)}, device_id_type=MESH,
        )

    def cot_copy(d, slot):
        return pltpu.make_async_remote_copy(
            cot.at[slot], cot.at[slot], cot_s.at[d], cot_r.at[d],
            device_id={"mp": lax.rem(mm_i + d, mp)}, device_id_type=MESH,
        )

    halo = [halo_copy(0), halo_copy(1)]
    for c in halo:
        c.start()
    each(n - 1, lambda d: mix_copy(d + 1).start())
    for d in range(1, mp):
        cot_copy(d, mm_i).start()

    lane = iota((1, width), 1)

    def per_tile(values):
        result = jnp.zeros(values[0].shape, F32)
        for t in range(tiles):
            result = jnp.where(lane == t, values[t], result)
        return result.astype(BF)

    def flag(x):
        return jnp.where(x > 0, 0.0, MASKED)

    for u in range(tiles):
        bias[u * tile : (u + 1) * tile, :] = per_tile(
            [jnp.full((tile, width), flag(lmask[t, u]), F32) for t in range(tiles)]
        )
    row_c = iota((cap, width), 0)
    for side in range(2):
        start = rows + side * cap
        bias[start : start + cap, :] = per_tile(
            [
                jnp.where(row_c < live[0, side], flag(lmask[t, tiles + side]), MASKED)
                for t in range(tiles)
            ]
        )
    row_m = iota((blk, width), 0)

    def mix_mask(d):
        source = lax.rem(me + n - d, n)
        values = []
        for t in range(tiles):
            inner = jnp.where(row_m < vn + slots, flag(emask[t, source]), MASKED)
            values.append(jnp.where(row_m < vn, 0.0, inner))
        bias[pl.ds(mix0 + d * blk, blk), :] = per_tile(values)

    each(n, mix_mask)

    feature = iota((width, rows), 0)

    def blocks(x):
        parts = []
        for h in range(heads):
            mine = (feature >= h * hd) & (feature < (h + 1) * hd)
            parts.append(jnp.where(mine, x, 0.0))
        return jnp.concatenate(parts, axis=1).astype(BF)

    loads[6].wait()
    q_t = jnp.transpose(q_v[...].astype(F32)) * (hd ** -0.5)
    q_blocks = blocks(q_t)
    col = iota((width, cols), 1)
    for h in range(1, heads):
        col = jnp.where(iota((width, cols), 1) >= h * rows, iota((width, cols), 1) - h * rows, col)
    tile_of = jnp.zeros((width, cols), jnp.int32)
    for t in range(1, tiles):
        tile_of = jnp.where(col >= t * tile, t, tile_of)
    in_tile = jnp.where(iota((width, cols), 0) == tile_of, 1.0, 0.0).astype(BF)
    q_aug = jnp.concatenate([q_blocks, in_tile], axis=0)

    chunks = [(0, rows), (rows, 2 * cap)]
    step_rows = min(n * blk, 256)
    chunks += [(mix0 + i, step_rows) for i in range(0, n * blk, step_rows)]

    def score(c):
        a, size = c
        keys = jnp.concatenate([kv[a : a + size, :width], bias[a : a + size, :]], axis=1)
        s = mm(keys, q_aug, NN)
        e_ref[a : a + size, :] = s
        return jnp.max(s, axis=0, keepdims=True)

    top = score(chunks[0])

    loads[7].wait()
    for d in range(1, mp):
        cot_copy(d, lax.rem(mm_i + mp - d, mp)).wait_recv()
    g_t = mm(w_v[...], jnp.concatenate([cot[i] for i in range(mp)], axis=1), NT)
    g_t = g_t.astype(BF).astype(F32)
    g_blocks = blocks(g_t)

    for c in halo:
        c.wait_recv()
    top = jnp.maximum(top, score(chunks[1]))
    each(n - 1, lambda d: mix_copy(d + 1).wait_recv())
    for c in chunks[2:]:
        top = jnp.maximum(top, score(c))

    norm = jnp.zeros((1, cols), F32)
    for a, size in chunks:
        e = jnp.exp(e_ref[a : a + size, :] - top)
        e_ref[a : a + size, :] = e
        norm = norm + jnp.sum(e, axis=0, keepdims=True)
    inv = 1.0 / norm
    for a, size in chunks:
        p = e_ref[a : a + size, :] * inv
        e_ref[a : a + size, :] = p
        pb_ref[a : a + size, :] = p.astype(BF)

    v_t = jnp.transpose(kv[:, width:])
    attn_t = jnp.concatenate(
        [
            mm(v_t[h * hd : (h + 1) * hd, :], pb_ref[:, h * rows : (h + 1) * rows], NN)
            for h in range(heads)
        ],
        axis=0,
    )
    attn_t = attn_t.astype(BF).astype(F32)
    prod = g_t * attn_t
    delta = jnp.concatenate(
        [jnp.sum(prod[h * hd : (h + 1) * hd, :], axis=0, keepdims=True) for h in range(heads)],
        axis=1,
    )
    attn = jnp.transpose(attn_t).astype(BF)

    def proj_copy(d):
        peer = lax.rem(mm_i + d, mp)
        return pltpu.make_async_remote_copy(
            proj.at[peer], proj_in.at[d], proj_s.at[d], proj_r.at[d],
            device_id={"mp": peer}, device_id_type=MESH,
        )

    full = mm(attn, w_v[...], NN)
    for i in range(mp):
        proj[i] = full[:, i * width : (i + 1) * width].astype(BF)
    for d in range(1, mp):
        proj_copy(d).start()
    mine = mm(attn, w_v[:, pl.ds(pl.multiple_of(mm_i * width, width), width)], NN)

    def backward(c):
        a, size = c
        dp = mm(kv[a : a + size, width:], g_blocks, NN)
        ds = (e_ref[a : a + size, :] * (dp - delta)).astype(BF)
        ds_ref[a : a + size, :] = ds
        gk = mm(ds, q_blocks, NT)
        gv = mm(pb_ref[a : a + size, :], g_blocks, NT)
        return gk, gv

    def halo_home(side):
        return pltpu.make_async_remote_copy(
            gback.at[side * cap : (side + 1) * cap, :], ret_halo.at[side],
            hb_s.at[side], hb_r.at[side],
            device_id={"nodes": left if side == 0 else right}, device_id_type=MESH,
        )

    def mix_home(d):
        return pltpu.make_async_remote_copy(
            gback.at[pl.ds(2 * cap + d * blk, blk), :], ret_mix.at[pl.ds(d * blk, blk), :],
            mb_s.at[d], mb_r.at[d],
            device_id={"nodes": lax.rem(me + n - d, n)}, device_id_type=MESH,
        )

    gk, gv = backward(chunks[1])
    gback[: 2 * cap, :width] = gk.astype(BF)
    gback[: 2 * cap, width:] = gv.astype(BF)
    home = [halo_home(0), halo_home(1)]
    for c in home:
        c.start()
    for c in chunks[2:]:
        gk, gv = backward(c)
        a = c[0] - rows
        gback[a : a + c[1], :width] = gk.astype(BF)
        gback[a : a + c[1], width:] = gv.astype(BF)
    each(n - 1, lambda d: mix_home(d + 1).start())
    gk, gv = backward(chunks[0])
    own_v[:, :width] = gk
    own_v[:, width:] = gv
    ret_mix[:blk, :] = gback[2 * cap : 2 * cap + blk, :]

    k_t = jnp.transpose(kv[:, :width])
    gq_t = jnp.concatenate(
        [
            mm(k_t[h * hd : (h + 1) * hd, :], ds_ref[:, h * rows : (h + 1) * rows], NN)
            for h in range(heads)
        ],
        axis=0,
    )
    gq_v[...] = jnp.transpose(gq_t * (hd ** -0.5))
    stores = [pltpu.make_async_copy(gq_v, gq_hbm, out_sem.at[0])]
    stores[-1].start()

    for d in range(1, mp):
        proj_copy(d).wait_recv()
        mine = mine + proj_in[d].astype(F32)
    out_v[...] = mine.astype(BF)
    stores.append(pltpu.make_async_copy(out_v, out_hbm, out_sem.at[1]))
    stores[-1].start()

    for c in home:
        c.wait_recv()
    acc = own_v[...] + mm(g_right, ret_halo[0], NN) + mm(g_left, ret_halo[1], NN)
    each(n - 1, lambda d: mix_home(d + 1).wait_recv())
    acc = acc + mm(onehot[...], ret_mix[...], TN)
    gk_v[...] = acc[:, :width]
    gv_v[...] = acc[:, width:]
    virt = jnp.sum(ret_mix[...].astype(F32).reshape(n, blk, 2 * width), axis=0)
    gvk_v[...] = virt[:vn, :width]
    gvv_v[...] = virt[:vn, width:]
    for i, (src, dst) in enumerate(
        ((gk_v, gk_hbm), (gv_v, gv_hbm), (gvk_v, gvk_hbm), (gvv_v, gvv_hbm))
    ):
        stores.append(pltpu.make_async_copy(src, dst, out_sem.at[2 + i]))
        stores[-1].start()

    for c in halo + home:
        c.wait_send()
    each(n - 1, lambda d: mix_copy(d + 1).wait_send())
    each(n - 1, lambda d: mix_home(d + 1).wait_send())
    for d in range(1, mp):
        cot_copy(d, mm_i).wait_send()
        proj_copy(d).wait_send()
    for c in stores:
        c.wait()


def solution(mesh):
    n, mp = mesh.shape["nodes"], mesh.shape["mp"]
    heads = HEADS // mp

    def step(q, k, v, w, cot, vk, vv, hrows, live, erows, lmask, emask):
        rows, width = q.shape
        cap, slots, vn = hrows.shape[2], erows.shape[2], vk.shape[0]
        blk = -(-(vn + slots) // 16) * 16
        total = rows + 2 * cap + n * blk
        smem = pl.BlockSpec(memory_space=pltpu.SMEM)
        hbm = pl.BlockSpec(memory_space=pl.ANY)
        dma = pltpu.SemaphoreType.DMA
        flops = 2 * total * rows * width * 5
        return pl.pallas_call(
            functools.partial(kernel, n, mp, heads),
            out_shape=(
                jax.ShapeDtypeStruct((rows, width), BF),
                jax.ShapeDtypeStruct((rows, width), F32),
                jax.ShapeDtypeStruct((rows, width), F32),
                jax.ShapeDtypeStruct((rows, width), F32),
                jax.ShapeDtypeStruct((vn, width), F32),
                jax.ShapeDtypeStruct((vn, width), F32),
            ),
            in_specs=[smem] * 4 + [hbm] * 8,
            out_specs=(hbm,) * 6,
            scratch_shapes=[
                pltpu.VMEM((rows, width), BF),
                pltpu.VMEM(w.shape, BF),
                pltpu.VMEM((vn, width), BF),
                pltpu.VMEM((vn, width), BF),
                pltpu.VMEM(hrows.shape, jnp.int32),
                pltpu.VMEM((total, 2 * width), BF),
                pltpu.VMEM((mp, rows, width), BF),
                pltpu.VMEM((total, width), BF),
                pltpu.VMEM((n * blk, rows), BF),
                pltpu.VMEM((n * blk, 2 * width), BF),
                pltpu.VMEM((2, cap, 2 * width), BF),
                pltpu.VMEM((total, heads * rows), F32),
                pltpu.VMEM((total, heads * rows), BF),
                pltpu.VMEM((total, heads * rows), BF),
                pltpu.VMEM((2 * cap + n * blk, 2 * width), BF),
                pltpu.VMEM((2, cap, 2 * width), BF),
                pltpu.VMEM((n * blk, 2 * width), BF),
                pltpu.VMEM((mp, rows, width), BF),
                pltpu.VMEM((mp, rows, width), BF),
                pltpu.VMEM((rows, 2 * width), F32),
                pltpu.VMEM((rows, width), BF),
                pltpu.VMEM((rows, width), F32),
                pltpu.VMEM((rows, width), F32),
                pltpu.VMEM((rows, width), F32),
                pltpu.VMEM((vn, width), F32),
                pltpu.VMEM((vn, width), F32),
                dma((8,)), dma((6,)),
                dma((2,)), dma((2,)), dma((n,)), dma((n,)),
                dma((mp,)), dma((mp,)), dma((mp,)), dma((mp,)),
                dma((2,)), dma((2,)), dma((n,)), dma((n,)),
            ],
            compiler_params=pltpu.CompilerParams(
                collective_id=0, has_side_effects=True, vmem_limit_bytes=48 << 20
            ),
            cost_estimate=pl.CostEstimate(
                flops=flops, transcendentals=total * rows * heads, bytes_accessed=2 << 20
            ),
        )(live, erows, lmask, emask, q, k, v, w, cot, vk, vv, hrows)

    node = P("nodes", "mp")
    return jax.shard_map(
        step,
        mesh=mesh,
        in_specs=(
            node, node, node, P("mp", None), node, node, node,
            P("nodes", None, None), P("nodes", None), P("nodes", None, None),
            P("nodes", None), P("nodes", None),
        ),
        out_specs=(node,) * 6,
        check_vma=False,
    )
```

time: 193 us -> 31.5 us (0.16)
  waiting for transfers between devices: 69.2 us -> 0 us
  blocking collectives: 57.9 us -> 0 us
  starting transfers between devices: 20.4 us -> 0 us
  Pallas kernels: 0 us -> 19.6 us
  between operations: 16.5 us -> 0.68 us
  other arithmetic: 8.82 us -> 0 us
  matrix products: 4.52 us -> 0 us
  local copies, waits for them, and re-layouts: 14.7 us -> 10.8 us
    unnamed x3 -> x0, waiting for transfers between devices: 69.2 us -> none
    all_gather x3 -> x0, blocking collectives: 57.9 us -> none  [the longest x1 26.1 us: body(): lax.all_gather(virtual_key, 'nodes', axis=0, tiled=True)]
    pallas_call x0 -> x1, Pallas kernels: none -> 19.6 us  [step(): pl.pallas_call(functools.partial(kernel, n, mp, heads), out_shape=(jax.Sh...]
    all_to_all x2 -> x0, starting transfers between devices: 10.7 us -> none  [the longest x1 7.41 us: body(): lax.all_to_all(expand_sent, 'nodes', split_axis=0, concat_axis=0, tiled=T...]
    ppermute x4 -> x0, starting transfers between devices: 9.52 us -> none  [the longest x2 7.45 us: extended(): after = lax.ppermute(leading, axis, down)]
    dot_general x14 -> x0, matrix products: 4.52 us -> none  [the longest x1 1.04 us: body(): projected = jnp.dot(attn, out_weight, preferred_element_type=jnp.float32)]
    scatter-add x3 -> x0, other arithmetic: 3.61 us -> none  [the longest x1 1.4 us: body(): own_grads = own_grads.at[to_left].add(for_left_sent)]
    gather x3 -> x0, local copies, waits for them, and re-layouts: 2.28 us -> none  [the longest x1 0.85 us: body(): key_value[to_right]]
  transfers between devices with their start and end apart: 8 -> 0, of which waited for: 1 -> 0; matrix products, arithmetic and copies ran while one was open for 8% -> 0% of each run, Pallas kernels for 0% -> 0%
where the time goes in v1:
time: 31.5 us; the launch traced here: 31.2 us
  Pallas kernels  19.6 us (62%)
  local copies, waits for them, and re-layouts  10.8 us (34%)
  between operations  0.68 us (2%)
    pallas_call x1, Pallas kernels, step(): pl.pallas_call(functools.partial(kernel, n, mp, heads), out_shape=(jax.Sh...  19.6 us
    unnamed x29, local copies, waits for them, and re-layouts  10.8 us

profile of v1, /device:TPU:0, one launch (start us, length us, event | category | flops | bytes accessed | tf_op | source)
XLA Modules:
  0.0 31.2 jit_solution(7990433124824718255)
XLA Ops:
  0.6 0.0 copy-start.7
  0.6 0.0 copy-start.6
  0.7 0.0 copy-start.5
  0.7 0.8 %copy.18.erows = s32[1,8,2]{2,1,0:T(8,128)S(1)} copy(s32[1,8,2]{1,2,0:T(2,128)} %param.21) | data formatting | bytes 128 | tf_op args[9]
  1.4 0.0 copy-done.7
  1.4 0.0 copy-done.6
  1.4 0.0 copy-done.5
  1.4 0.0 copy-start
  1.4 0.9 %copy-done = bf16[128,512]{1,0:T(8,128)(2,1)S(1)} copy-done((bf16[128,512]{1,0:T(8,128)(2,1)S(1)}, bf16[128,512]{1,0:T(8,128)(2,1)}, u32[]{:S(2)}) %copy-start) | copy-done | bytes 131096
  2.3 0.0 copy-start.1
  2.4 0.8 %copy-done.1 = bf16[256,128]{1,0:T(8,128)(2,1)S(1)} copy-done((bf16[256,128]{1,0:T(8,128)(2,1)S(1)}, bf16[256,128]{1,0:T(8,128)(2,1)}, u32[]{:S(2)}) %copy-start.1) | copy-done | bytes 65560
  3.2 0.0 copy-start.2
  3.2 0.8 %copy-done.2 = bf16[256,128]{1,0:T(8,128)(2,1)S(1)} copy-done((bf16[256,128]{1,0:T(8,128)(2,1)S(1)}, bf16[256,128]{1,0:T(8,128)(2,1)}, u32[]{:S(2)}) %copy-start.2) | copy-done | bytes 65560
  4.0 0.0 copy-start.3
  4.0 0.8 %copy-done.3 = bf16[256,128]{1,0:T(8,128)(2,1)S(1)} copy-done((bf16[256,128]{1,0:T(8,128)(2,1)S(1)}, bf16[256,128]{1,0:T(8,128)(2,1)}, u32[]{:S(2)}) %copy-start.3) | copy-done | bytes 65560
  4.9 0.0 copy-start.4
  4.9 0.8 %copy-done.4 = bf16[256,128]{1,0:T(8,128)(2,1)S(1)} copy-done((bf16[256,128]{1,0:T(8,128)(2,1)S(1)}, bf16[256,128]{1,0:T(8,128)(2,1)}, u32[]{:S(2)}) %copy-start.4) | copy-done | bytes 65560
  5.7 0.0 copy-start.8
  5.7 0.7 %copy-done.8 = s32[2,8]{1,0:T(2,128)S(1)} copy-done((s32[2,8]{1,0:T(2,128)S(1)}, s32[2,8]{1,0:T(2,128)}, u32[]{:S(2)}) %copy-start.8) | copy-done | bytes 88
  6.4 0.0 copy-start.9
  6.4 0.7 %copy-done.9 = s32[1,2,128]{2,1,0:T(2,128)S(1)} copy-done((s32[1,2,128]{2,1,0:T(2,128)S(1)}, s32[1,2,128]{2,1,0:T(2,128)}, u32[]{:S(2)}) %copy-start.9) | copy-done | bytes 1048
  7.1 0.0 copy-start.10
  7.1 0.7 %copy-done.10 = s32[1,2]{1,0:T(1,128)S(1)} copy-done((s32[1,2]{1,0:T(1,128)S(1)}, s32[1,2]{1,0:T(1,128)}, u32[]{:S(2)}) %copy-start.10) | copy-done | bytes 32
  7.7 19.6 %shard_map.163 = (bf16[256,128]{1,0:T(8,128)(2,1)S(1)}, f32[256,128]{1,0:T(8,128)S(1)}, f32[256,128]{1,0:T(8,128)S(1)}, f32[256,128]{1,0:T(8,128)S(1)}, f32[8,128]{1,0:T(8,128)S(1)}, /*index=5*/f32[8,128]{1,0:T(8,128)S(1)}) custom-call(s32[1,2]{1,0:T(1,128)S(1)} %copy-done.10, s32[1,8,2]{2,1,0:T(8,128)S(1)} %copy.18.erows, s32[2,4]{1,0:T(2,128)S(1)} %copy-done.7, ...), custom_call_target="tpu_custom_call" | custom-call | flops 209715200 | bytes 2097152 | tf_op jit(solution)/shard_map/pallas_call | solution.py:368
  27.4 0.6 %copy.25 = bf16[256,128]{1,0:T(8,128)(2,1)} copy(bf16[256,128]{1,0:T(8,128)(2,1)S(1)} %get-tuple-element.12) | data formatting | bytes 131072
  28.0 0.7 %copy.26 = f32[256,128]{1,0:T(8,128)} copy(f32[256,128]{1,0:T(8,128)S(1)} %get-tuple-element.13) | data formatting | bytes 262144
  28.7 0.7 %copy.27 = f32[256,128]{1,0:T(8,128)} copy(f32[256,128]{1,0:T(8,128)S(1)} %get-tuple-element.14) | data formatting | bytes 262144
  29.3 0.7 %copy.28 = f32[256,128]{1,0:T(8,128)} copy(f32[256,128]{1,0:T(8,128)S(1)} %get-tuple-element.15) | data formatting | bytes 262144
  30.0 0.6 %copy.29 = f32[8,128]{1,0:T(8,128)} copy(f32[8,128]{1,0:T(8,128)S(1)} %get-tuple-element.16) | data formatting | bytes 8192
  30.6 0.6 %copy.30 = f32[8,128]{1,0:T(8,128)} copy(f32[8,128]{1,0:T(8,128)S(1)} %get-tuple-element.17) | data formatting | bytes 8192
Async XLA Ops:
  0.6 0.8 %copy-start.7 = (s32[2,4]{1,0:T(2,128)S(1)}, s32[2,4]{1,0:T(2,128)}, u32[]{:S(2)}) copy-start(s32[2,4]{1,0:T(2,128)} %lmask.1) | copy-start | bytes 100
  0.6 0.8 %copy-start.6 = (bf16[8,128]{1,0:T(8,128)(2,1)S(1)}, bf16[8,128]{1,0:T(8,128)(2,1)}, u32[]{:S(2)}) copy-start(bf16[8,128]{1,0:T(8,128)(2,1)} %vv_hbm.1) | copy-start | bytes 6148
  0.7 0.8 %copy-start.5 = (bf16[8,128]{1,0:T(8,128)(2,1)S(1)}, bf16[8,128]{1,0:T(8,128)(2,1)}, u32[]{:S(2)}) copy-start(bf16[8,128]{1,0:T(8,128)(2,1)} %vk_hbm.1) | copy-start | bytes 6148
  1.4 0.9 %copy-start = (bf16[128,512]{1,0:T(8,128)(2,1)S(1)}, bf16[128,512]{1,0:T(8,128)(2,1)}, u32[]{:S(2)}) copy-start(bf16[128,512]{1,0:T(8,128)(2,1)} %w_hbm.1) | copy-start | bytes 393220
  2.3 0.8 %copy-start.1 = (bf16[256,128]{1,0:T(8,128)(2,1)S(1)}, bf16[256,128]{1,0:T(8,128)(2,1)}, u32[]{:S(2)}) copy-start(bf16[256,128]{1,0:T(8,128)(2,1)} %q_hbm.1) | copy-start | bytes 196612
  3.2 0.8 %copy-start.2 = (bf16[256,128]{1,0:T(8,128)(2,1)S(1)}, bf16[256,128]{1,0:T(8,128)(2,1)}, u32[]{:S(2)}) copy-start(bf16[256,128]{1,0:T(8,128)(2,1)} %k_hbm.1) | copy-start | bytes 196612
  4.0 0.8 %copy-start.3 = (bf16[256,128]{1,0:T(8,128)(2,1)S(1)}, bf16[256,128]{1,0:T(8,128)(2,1)}, u32[]{:S(2)}) copy-start(bf16[256,128]{1,0:T(8,128)(2,1)} %v_hbm.1) | copy-start | bytes 196612
  4.9 0.8 %copy-start.4 = (bf16[256,128]{1,0:T(8,128)(2,1)S(1)}, bf16[256,128]{1,0:T(8,128)(2,1)}, u32[]{:S(2)}) copy-start(bf16[256,128]{1,0:T(8,128)(2,1)} %cot_hbm.1) | copy-start | bytes 196612
  5.7 0.7 %copy-start.8 = (s32[2,8]{1,0:T(2,128)S(1)}, s32[2,8]{1,0:T(2,128)}, u32[]{:S(2)}) copy-start(s32[2,8]{1,0:T(2,128)} %emask.1) | copy-start | bytes 196
  6.4 0.7 %copy-start.9 = (s32[1,2,128]{2,1,0:T(2,128)S(1)}, s32[1,2,128]{2,1,0:T(2,128)}, u32[]{:S(2)}) copy-start(s32[1,2,128]{2,1,0:T(2,128)} %hrows_hbm.1) | copy-start | bytes 3076
  7.1 0.7 %copy-start.10 = (s32[1,2]{1,0:T(1,128)S(1)}, s32[1,2]{1,0:T(1,128)}, u32[]{:S(2)}) copy-start(s32[1,2]{1,0:T(1,128)} %live.1) | copy-start | bytes 28

commit v2 on v1

--- a/solution.py
+++ b/solution.py
@@ -36,10 +36,10 @@
 
 def kernel(
     n, mp, heads,
-    live, erows, lmask, emask,
+    live_hbm, erows_hbm, lmask_hbm, emask_hbm,
     q_hbm, k_hbm, v_hbm, w_hbm, cot_hbm, vk_hbm, vv_hbm, hrows_hbm,
     out_hbm, gq_hbm, gk_hbm, gv_hbm, gvk_hbm, gvv_hbm,
-    q_v, w_v, vk_v, vv_v, hrows, kv, cot, bias, onehot, mix_send, halo_send,
+    live, erows, lmask, emask, q_v, w_v, vk_v, vv_v, hrows, kv, cot, bias, onehot, mix_send, halo_send,
     e_ref, pb_ref, ds_ref, gback, ret_halo, ret_mix, proj, proj_in, own_v,
     out_v, gq_v, gk_v, gv_v, gvk_v, gvv_v,
     in_sem, out_sem, halo_s, halo_r, mix_s, mix_r, cot_s, cot_r, proj_s, proj_r,
@@ -51,7 +51,7 @@
     tiles = lmask.shape[0]
     tile = rows // tiles
     cap = hrows.shape[2]
-    slots = erows.shape[2]
+    slots = erows.shape[1]
     vn = vk_v.shape[0]
     blk = ret_mix.shape[0] // n
     hd = width // heads
@@ -73,6 +73,14 @@
             barrier, inc=1, device_id={"mp": lax.rem(mm_i + d, mp)}, device_id_type=MESH
         )
 
+    small = [
+        pltpu.make_async_copy(src, dst, in_sem.at[8 + i])
+        for i, (src, dst) in enumerate(
+            ((erows_hbm, erows), (live_hbm, live), (lmask_hbm, lmask), (emask_hbm, emask))
+        )
+    ]
+    for c in small:
+        c.start()
     loads = [
         pltpu.make_async_copy(k_hbm, kv.at[:rows, :width], in_sem.at[0]),
         pltpu.make_async_copy(v_hbm, kv.at[:rows, width:], in_sem.at[1]),
@@ -92,9 +100,10 @@
         peer = lax.rem(me + d, n)
         target = jnp.full((blk, rows), -1, jnp.int32)
         for s in range(slots):
-            target = jnp.where(row_b == vn + s, erows[0, peer, s], target)
+            target = jnp.where(row_b == vn + s, erows[0, s, peer], target)
         onehot[pl.ds(d * blk, blk), :] = jnp.where(lane_b == target, 1.0, 0.0).astype(BF)
 
+    small[0].wait()
     each(n, fill)
 
     for c in loads[:5]:
@@ -140,6 +149,9 @@
     each(n - 1, lambda d: mix_copy(d + 1).start())
     for d in range(1, mp):
         cot_copy(d, mm_i).start()
+
+    for c in small[1:]:
+        c.wait()
 
     lane = iota((1, width), 1)
 
@@ -352,6 +364,15 @@
         c.wait()
 
 
+def hand_over(*refs):
+    sem = refs[-1]
+    copies = [pltpu.make_async_copy(refs[i], refs[6 + i], sem.at[i]) for i in range(6)]
+    for c in copies:
+        c.start()
+    for c in copies:
+        c.wait()
+
+
 def solution(mesh):
     n, mp = mesh.shape["nodes"], mesh.shape["mp"]
     heads = HEADS // mp
@@ -361,11 +382,17 @@
         cap, slots, vn = hrows.shape[2], erows.shape[2], vk.shape[0]
         blk = -(-(vn + slots) // 16) * 16
         total = rows + 2 * cap + n * blk
-        smem = pl.BlockSpec(memory_space=pltpu.SMEM)
-        hbm = pl.BlockSpec(memory_space=pl.ANY)
+        hbm = pl.BlockSpec(memory_space=pltpu.HBM)
+        anywhere = pl.BlockSpec(memory_space=pl.ANY)
+        erows = jnp.swapaxes(erows, 1, 2)
+        smalls = [pltpu.SMEM(x.shape, jnp.int32) for x in (live, erows, lmask, emask)]
         dma = pltpu.SemaphoreType.DMA
         flops = 2 * total * rows * width * 5
-        return pl.pallas_call(
+        operands = [
+            pltpu.with_memory_space_constraint(x, pltpu.HBM)
+            for x in (live, erows, lmask, emask, q, k, v, w, cot, vk, vv, hrows)
+        ]
+        results = pl.pallas_call(
             functools.partial(kernel, n, mp, heads),
             out_shape=(
                 jax.ShapeDtypeStruct((rows, width), BF),
@@ -375,9 +402,9 @@
                 jax.ShapeDtypeStruct((vn, width), F32),
                 jax.ShapeDtypeStruct((vn, width), F32),
             ),
-            in_specs=[smem] * 4 + [hbm] * 8,
-            out_specs=(hbm,) * 6,
-            scratch_shapes=[
+            in_specs=[hbm] * 12,
+            out_specs=(anywhere,) * 6,
+            scratch_shapes=smalls + [
                 pltpu.VMEM((rows, width), BF),
                 pltpu.VMEM(w.shape, BF),
                 pltpu.VMEM((vn, width), BF),
@@ -404,18 +431,25 @@
                 pltpu.VMEM((rows, width), F32),
                 pltpu.VMEM((vn, width), F32),
                 pltpu.VMEM((vn, width), F32),
-                dma((8,)), dma((6,)),
+                dma((12,)), dma((6,)),
                 dma((2,)), dma((2,)), dma((n,)), dma((n,)),
                 dma((mp,)), dma((mp,)), dma((mp,)), dma((mp,)),
                 dma((2,)), dma((2,)), dma((n,)), dma((n,)),
             ],
             compiler_params=pltpu.CompilerParams(
-                collective_id=0, has_side_effects=True, vmem_limit_bytes=48 << 20
+                collective_id=0, has_side_effects=True, vmem_limit_bytes=62 << 20
             ),
             cost_estimate=pl.CostEstimate(
                 flops=flops, transcendentals=total * rows * heads, bytes_accessed=2 << 20
             ),
-        )(live, erows, lmask, emask, q, k, v, w, cot, vk, vv, hrows)
+        )(*operands)
+        return pl.pallas_call(
+            hand_over,
+            out_shape=tuple(jax.ShapeDtypeStruct(x.shape, x.dtype) for x in results),
+            in_specs=[anywhere] * 6,
+            out_specs=(hbm,) * 6,
+            scratch_shapes=[dma((6,))],
+        )(*results)
 
     node = P("nodes", "mp")
     return jax.shard_map(

time: 31.5 us -> 35.4 us (1.12)
  Pallas kernels: 19.6 us -> 34.6 us
  local copies, waits for them, and re-layouts: 10.8 us -> 0 us
    pallas_call x0 -> x1, Pallas kernels: none -> 15.3 us  [step(): pl.pallas_call(hand_over, out_shape=tuple((jax.ShapeDtypeStruct(x.shape,...]
    unnamed x29 -> x0, local copies, waits for them, and re-layouts: 10.8 us -> none
    pallas_call x1, Pallas kernels: 19.6 us -> 19.3 us  [step(): pl.pallas_call(functools.partial(kernel, n, mp, heads), out_shape=(jax.Sh...]
where the time goes in v2:
time: 35.4 us; the launch traced here: 35.2 us
  Pallas kernels  34.6 us (98%)
  between operations  0.64 us (2%)
    pallas_call x1, Pallas kernels, step(): pl.pallas_call(functools.partial(kernel, n, mp, heads), out_shape=(jax.Sh...  19.3 us
    pallas_call x1, Pallas kernels, step(): pl.pallas_call(hand_over, out_shape=tuple((jax.ShapeDtypeStruct(x.shape,...  15.3 us

profile of v2, /device:TPU:0, one launch (start us, length us, event | category | flops | bytes accessed | tf_op | source)
XLA Modules:
  0.0 35.2 jit_solution(13752970953188293184)
XLA Ops:
  0.6 19.3 %shard_map.163 = (bf16[256,128]{1,0:T(8,128)(2,1)}, f32[256,128]{1,0:T(8,128)}, f32[256,128]{1,0:T(8,128)}, f32[256,128]{1,0:T(8,128)}, f32[8,128]{1,0:T(8,128)}, /*index=5*/f32[8,128]{1,0:T(8,128)}) custom-call(s32[1,2]{1,0:T(1,128)} %live_hbm.1, s32[1,2,8]{2,1,0:T(2,128)} %bitcast.1, s32[2,4]{1,0:T(2,128)} %lmask_hbm.1, s32[2,8]{1,0:T(2,128)} %emask_hbm.1, ...), custom_call_target="tpu_custom_call" | custom-call | flops 209715200 | bytes 2097152 | tf_op jit(solution)/shard_map/pallas_call | solution.py:395
  19.9 15.3 %shard_map.164 = (bf16[256,128]{1,0:T(8,128)(2,1)}, f32[256,128]{1,0:T(8,128)}, f32[256,128]{1,0:T(8,128)}, f32[256,128]{1,0:T(8,128)}, f32[8,128]{1,0:T(8,128)}, /*index=5*/f32[8,128]{1,0:T(8,128)}) custom-call(bf16[256,128]{1,0:T(8,128)(2,1)} %get-tuple-element.12.refs_0_, f32[256,128]{1,0:T(8,128)} %get-tuple-element.13.refs_1_, ...), custom_call_target="tpu_custom_call" | custom-call | tf_op jit(solution)/shard_map/pallas_call | solution.py:446

commit v3 on v2

--- a/solution.py
+++ b/solution.py
@@ -437,7 +437,7 @@
                 dma((2,)), dma((2,)), dma((n,)), dma((n,)),
             ],
             compiler_params=pltpu.CompilerParams(
-                collective_id=0, has_side_effects=True, vmem_limit_bytes=62 << 20
+                collective_id=0, has_side_effects=True, vmem_limit_bytes=40 << 20
             ),
             cost_estimate=pl.CostEstimate(
                 flops=flops, transcendentals=total * rows * heads, bytes_accessed=2 << 20
@@ -449,6 +449,8 @@
             in_specs=[anywhere] * 6,
             out_specs=(hbm,) * 6,
             scratch_shapes=[dma((6,))],
+            compiler_params=pltpu.CompilerParams(vmem_limit_bytes=4 << 20),
+            cost_estimate=pl.CostEstimate(flops=0, transcendentals=0, bytes_accessed=1 << 20),
         )(*results)
 
     node = P("nodes", "mp")

time: 35.4 us -> 20.7 us (0.58)
  Pallas kernels: 34.6 us -> 19.9 us
    pallas_call x1, Pallas kernels: 15.3 us -> 0.82 us  [step(): pl.pallas_call(hand_over, out_shape=tuple((jax.ShapeDtypeStruct(x.shape,...]
where the time goes in v3:
time: 20.7 us; the launch traced here: 20.5 us
  Pallas kernels  19.9 us (96%)
  between operations  0.64 us (3%)
    pallas_call x1, Pallas kernels, step(): pl.pallas_call(functools.partial(kernel, n, mp, heads), out_shape=(jax.Sh...  19 us
    pallas_call x1, Pallas kernels, step(): pl.pallas_call(hand_over, out_shape=tuple((jax.ShapeDtypeStruct(x.shape,...  0.82 us

profile of v3, /device:TPU:0, one launch (start us, length us, event | category | flops | bytes accessed | tf_op | source)
XLA Modules:
  0.0 20.5 jit_solution(17854318204760493701)
XLA Ops:
  0.6 19.0 %shard_map.163 = (bf16[256,128]{1,0:T(8,128)(2,1)S(1)}, f32[256,128]{1,0:T(8,128)S(1)}, f32[256,128]{1,0:T(8,128)S(1)}, f32[256,128]{1,0:T(8,128)S(1)}, f32[8,128]{1,0:T(8,128)S(1)}, /*index=5*/f32[8,128]{1,0:T(8,128)S(1)}) custom-call(s32[1,2]{1,0:T(1,128)} %live_hbm.1, s32[1,2,8]{2,1,0:T(2,128)} %bitcast.1, s32[2,4]{1,0:T(2,128)} %lmask_hbm.1, ...), custom_call_target="tpu_custom_call" | custom-call | flops 209715200 | bytes 2097152 | tf_op jit(solution)/shard_map/pallas_call | solution.py:395
  19.7 0.8 %shard_map.164 = (bf16[256,128]{1,0:T(8,128)(2,1)}, f32[256,128]{1,0:T(8,128)}, f32[256,128]{1,0:T(8,128)}, f32[256,128]{1,0:T(8,128)}, f32[8,128]{1,0:T(8,128)}, /*index=5*/f32[8,128]{1,0:T(8,128)}) custom-call(bf16[256,128]{1,0:T(8,128)(2,1)S(1)} %get-tuple-element.12.refs_0_, f32[256,128]{1,0:T(8,128)S(1)} %get-tuple-element.13.refs_1_, ...), custom_call_target="tpu_custom_call" | custom-call | bytes 1048576 | tf_op jit(solution)/shard_map/pallas_call | solution.py:446

commit v4 on v3

--- a/solution.py
+++ b/solution.py
@@ -38,11 +38,10 @@
     n, mp, heads,
     live_hbm, erows_hbm, lmask_hbm, emask_hbm,
     q_hbm, k_hbm, v_hbm, w_hbm, cot_hbm, vk_hbm, vv_hbm, hrows_hbm,
-    out_hbm, gq_hbm, gk_hbm, gv_hbm, gvk_hbm, gvv_hbm,
+    out_v, gq_v, gk_v, gv_v, gvk_v, gvv_v,
     live, erows, lmask, emask, q_v, w_v, vk_v, vv_v, hrows, kv, cot, bias, onehot, mix_send, halo_send,
-    e_ref, pb_ref, ds_ref, gback, ret_halo, ret_mix, proj, proj_in, own_v,
-    out_v, gq_v, gk_v, gv_v, gvk_v, gvv_v,
-    in_sem, out_sem, halo_s, halo_r, mix_s, mix_r, cot_s, cot_r, proj_s, proj_r,
+    kvt, e_ref, pb_ref, ds_ref, gback, ret_halo, ret_mix, proj, proj_in, own_v,
+    in_sem, halo_s, halo_r, mix_s, mix_r, cot_s, cot_r, proj_s, proj_r,
     hb_s, hb_r, mb_s, mb_r,
 ):
     me = lax.axis_index("nodes")
@@ -106,50 +105,52 @@
     small[0].wait()
     each(n, fill)
 
-    for c in loads[:5]:
+    for c in loads[:3]:
         c.wait()
     own = kv[:rows, :]
-    g_right = jnp.where(iota((rows, cap), 0) == hrows[0, 0:1, :], 1.0, 0.0).astype(BF)
-    g_left = jnp.where(iota((rows, cap), 0) == hrows[0, 1:2, :], 1.0, 0.0).astype(BF)
-    halo_send[0] = mm(g_right, own, TN).astype(BF)
-    halo_send[1] = mm(g_left, own, TN).astype(BF)
+    wanted = jnp.concatenate([hrows[0].astype(F32), jnp.zeros((6, cap), F32)], axis=0)
+    wanted = jnp.transpose(wanted).astype(jnp.int32)
+    wanted = jnp.concatenate([wanted[:, 0:1], wanted[:, 1:2]], axis=0)
+    picks = jnp.where(iota((2 * cap, rows), 1) == wanted, 1.0, 0.0).astype(BF)
+    halo_send[...] = mm(picks, own, NN).astype(BF).reshape(2, cap, 2 * width)
+
+    pl.semaphore_wait(barrier, n - 1 + mp - 1)
+
+    def halo_copy(side):
+        start = rows + side * cap
+        return pltpu.make_async_remote_copy(
+            halo_send.at[side], kv.at[start : start + cap, :], halo_s.at[side], halo_r.at[side],
+            device_id={"nodes": right if side == 0 else left}, device_id_type=MESH,
+        )
+
+    def mix_copy(d):
+        return pltpu.make_async_remote_copy(
+            mix_send.at[pl.ds(d * blk, blk), :], kv.at[pl.ds(mix0 + d * blk, blk), :],
+            mix_s.at[d], mix_r.at[d],
+            device_id={"nodes": lax.rem(me + d, n)}, device_id_type=MESH,
+        )
+
+    def cot_copy(d, slot):
+        return pltpu.make_async_remote_copy(
+            cot.at[slot], cot.at[slot], cot_s.at[d], cot_r.at[d],
+            device_id={"mp": lax.rem(mm_i + d, mp)}, device_id_type=MESH,
+        )
+
+    halo = [halo_copy(0), halo_copy(1)]
+    for c in halo:
+        c.start()
+
+    for c in loads[3:6]:
+        c.wait()
     virt = jnp.concatenate([vk_v[...].astype(F32), vv_v[...].astype(F32)], axis=1)
     virt = jnp.concatenate([virt, jnp.zeros((blk - vn, 2 * width), F32)], axis=0)
     taken = mm(onehot[...], own, NN).reshape(n, blk, 2 * width) + virt[None]
     taken = taken.astype(BF)
     mix_send[...] = taken.reshape(n * blk, 2 * width)
+    each(n - 1, lambda d: mix_copy(d + 1).start())
+    for d in range(1, mp):
+        cot_copy(d, mm_i).start()
     kv[mix0 : mix0 + blk, :] = taken[0]
-    loads[5].wait()
-
-    pl.semaphore_wait(barrier, n - 1 + mp - 1)
-
-    def halo_copy(side):
-        start = rows + side * cap
-        return pltpu.make_async_remote_copy(
-            halo_send.at[side], kv.at[start : start + cap, :], halo_s.at[side], halo_r.at[side],
-            device_id={"nodes": right if side == 0 else left}, device_id_type=MESH,
-        )
-
-    def mix_copy(d):
-        return pltpu.make_async_remote_copy(
-            mix_send.at[pl.ds(d * blk, blk), :], kv.at[pl.ds(mix0 + d * blk, blk), :],
-            mix_s.at[d], mix_r.at[d],
-            device_id={"nodes": lax.rem(me + d, n)}, device_id_type=MESH,
-        )
-
-    def cot_copy(d, slot):
-        return pltpu.make_async_remote_copy(
-            cot.at[slot], cot.at[slot], cot_s.at[d], cot_r.at[d],
-            device_id={"mp": lax.rem(mm_i + d, mp)}, device_id_type=MESH,
-        )
-
-    halo = [halo_copy(0), halo_copy(1)]
-    for c in halo:
-        c.start()
-    each(n - 1, lambda d: mix_copy(d + 1).start())
-    for d in range(1, mp):
-        cot_copy(d, mm_i).start()
-
     for c in small[1:]:
         c.wait()
 
@@ -218,70 +219,73 @@
         a, size = c
         keys = jnp.concatenate([kv[a : a + size, :width], bias[a : a + size, :]], axis=1)
         s = mm(keys, q_aug, NN)
-        e_ref[a : a + size, :] = s
-        return jnp.max(s, axis=0, keepdims=True)
-
-    top = score(chunks[0])
-
-    loads[7].wait()
-    for d in range(1, mp):
-        cot_copy(d, lax.rem(mm_i + mp - d, mp)).wait_recv()
-    g_t = mm(w_v[...], jnp.concatenate([cot[i] for i in range(mp)], axis=1), NT)
-    g_t = g_t.astype(BF).astype(F32)
-    g_blocks = blocks(g_t)
-
+        top = jnp.max(s, axis=0, keepdims=True)
+        e = jnp.exp(s - top)
+        e_ref[a : a + size, :] = e
+        kvt[:, a : a + size] = jnp.transpose(kv[a : a + size, :])
+        return top, jnp.sum(e, axis=0, keepdims=True)
+
+    stats = [score(chunks[0])]
+    g_right = jnp.where(iota((rows, cap), 0) == hrows[0, 0:1, :], 1.0, 0.0).astype(BF)
+    g_left = jnp.where(iota((rows, cap), 0) == hrows[0, 1:2, :], 1.0, 0.0).astype(BF)
     for c in halo:
         c.wait_recv()
-    top = jnp.maximum(top, score(chunks[1]))
+    stats.append(score(chunks[1]))
     each(n - 1, lambda d: mix_copy(d + 1).wait_recv())
     for c in chunks[2:]:
-        top = jnp.maximum(top, score(c))
-
-    norm = jnp.zeros((1, cols), F32)
+        stats.append(score(c))
+
+    top = functools.reduce(jnp.maximum, [t for t, _ in stats])
+    factor = [jnp.exp(t - top) for t, _ in stats]
+    norm = sum(f * z for f, (_, z) in zip(factor, stats))
+    inv = 1.0 / norm
+    factor = {c: f * inv for c, f in zip(chunks, factor)}
     for a, size in chunks:
-        e = jnp.exp(e_ref[a : a + size, :] - top)
-        e_ref[a : a + size, :] = e
-        norm = norm + jnp.sum(e, axis=0, keepdims=True)
-    inv = 1.0 / norm
-    for a, size in chunks:
-        p = e_ref[a : a + size, :] * inv
-        e_ref[a : a + size, :] = p
-        pb_ref[a : a + size, :] = p.astype(BF)
-
-    v_t = jnp.transpose(kv[:, width:])
+        pb_ref[a : a + size, :] = (e_ref[a : a + size, :] * factor[(a, size)]).astype(BF)
+
     attn_t = jnp.concatenate(
         [
-            mm(v_t[h * hd : (h + 1) * hd, :], pb_ref[:, h * rows : (h + 1) * rows], NN)
+            mm(
+                kvt[width + h * hd : width + (h + 1) * hd, :],
+                pb_ref[:, h * rows : (h + 1) * rows],
+                NN,
+            )
             for h in range(heads)
         ],
         axis=0,
     )
     attn_t = attn_t.astype(BF).astype(F32)
+    loads[7].wait()
+    attn = jnp.transpose(attn_t).astype(BF)
+
+    def proj_copy(d):
+        peer = lax.rem(mm_i + d, mp)
+        return pltpu.make_async_remote_copy(
+            proj.at[peer], proj_in.at[d], proj_s.at[d], proj_r.at[d],
+            device_id={"mp": peer}, device_id_type=MESH,
+        )
+
+    full = mm(attn, w_v[...], NN)
+    for i in range(mp):
+        proj[i] = full[:, i * width : (i + 1) * width].astype(BF)
+    for d in range(1, mp):
+        proj_copy(d).start()
+
+    for d in range(1, mp):
+        cot_copy(d, lax.rem(mm_i + mp - d, mp)).wait_recv()
+    g_t = mm(w_v[...], jnp.concatenate([cot[i] for i in range(mp)], axis=1), NT)
+    g_t = g_t.astype(BF).astype(F32)
+    g_blocks = blocks(g_t)
     prod = g_t * attn_t
     delta = jnp.concatenate(
         [jnp.sum(prod[h * hd : (h + 1) * hd, :], axis=0, keepdims=True) for h in range(heads)],
         axis=1,
     )
-    attn = jnp.transpose(attn_t).astype(BF)
-
-    def proj_copy(d):
-        peer = lax.rem(mm_i + d, mp)
-        return pltpu.make_async_remote_copy(
-            proj.at[peer], proj_in.at[d], proj_s.at[d], proj_r.at[d],
-            device_id={"mp": peer}, device_id_type=MESH,
-        )
-
-    full = mm(attn, w_v[...], NN)
-    for i in range(mp):
-        proj[i] = full[:, i * width : (i + 1) * width].astype(BF)
-    for d in range(1, mp):
-        proj_copy(d).start()
-    mine = mm(attn, w_v[:, pl.ds(pl.multiple_of(mm_i * width, width), width)], NN)
 
     def backward(c):
         a, size = c
         dp = mm(kv[a : a + size, width:], g_blocks, NN)
-        ds = (e_ref[a : a + size, :] * (dp - delta)).astype(BF)
+        ds = (e_ref[a : a + size, :] * factor[c] * (dp - delta)).astype(BF)
         ds_ref[a : a + size, :] = ds
         gk = mm(ds, q_blocks, NT)
         gv = mm(pb_ref[a : a + size, :], g_blocks, NT)
@@ -318,24 +322,20 @@
     own_v[:, width:] = gv
     ret_mix[:blk, :] = gback[2 * cap : 2 * cap + blk, :]
 
-    k_t = jnp.transpose(kv[:, :width])
     gq_t = jnp.concatenate(
         [
-            mm(k_t[h * hd : (h + 1) * hd, :], ds_ref[:, h * rows : (h + 1) * rows], NN)
+            mm(kvt[h * hd : (h + 1) * hd, :], ds_ref[:, h * rows : (h + 1) * rows], NN)
             for h in range(heads)
         ],
         axis=0,
     )
     gq_v[...] = jnp.transpose(gq_t * (hd ** -0.5))
-    stores = [pltpu.make_async_copy(gq_v, gq_hbm, out_sem.at[0])]
-    stores[-1].start()
-
+
+    mine = mm(attn, w_v[:, pl.ds(pl.multiple_of(mm_i * width, width), width)], NN)
     for d in range(1, mp):
         proj_copy(d).wait_recv()
         mine = mine + proj_in[d].astype(F32)
     out_v[...] = mine.astype(BF)
-    stores.append(pltpu.make_async_copy(out_v, out_hbm, out_sem.at[1]))
-    stores[-1].start()
 
     for c in home:
         c.wait_recv()
@@ -347,12 +347,6 @@
     virt = jnp.sum(ret_mix[...].astype(F32).reshape(n, blk, 2 * width), axis=0)
     gvk_v[...] = virt[:vn, :width]
     gvv_v[...] = virt[:vn, width:]
-    for i, (src, dst) in enumerate(
-        ((gk_v, gk_hbm), (gv_v, gv_hbm), (gvk_v, gvk_hbm), (gvv_v, gvv_hbm))
-    ):
-        stores.append(pltpu.make_async_copy(src, dst, out_sem.at[2 + i]))
-        stores[-1].start()
-
     for c in halo + home:
         c.wait_send()
     each(n - 1, lambda d: mix_copy(d + 1).wait_send())
@@ -360,8 +354,6 @@
     for d in range(1, mp):
         cot_copy(d, mm_i).wait_send()
         proj_copy(d).wait_send()
-    for c in stores:
-        c.wait()
 
 
 def hand_over(*refs):
@@ -403,7 +395,7 @@
                 jax.ShapeDtypeStruct((vn, width), F32),
             ),
             in_specs=[hbm] * 12,
-            out_specs=(anywhere,) * 6,
+            out_specs=(pl.BlockSpec(memory_space=pltpu.VMEM),) * 6,
             scratch_shapes=smalls + [
                 pltpu.VMEM((rows, width), BF),
                 pltpu.VMEM(w.shape, BF),
@@ -416,6 +408,7 @@
                 pltpu.VMEM((n * blk, rows), BF),
                 pltpu.VMEM((n * blk, 2 * width), BF),
                 pltpu.VMEM((2, cap, 2 * width), BF),
+                pltpu.VMEM((2 * width, total), BF),
                 pltpu.VMEM((total, heads * rows), F32),
                 pltpu.VMEM((total, heads * rows), BF),
                 pltpu.VMEM((total, heads * rows), BF),
@@ -425,13 +418,7 @@
                 pltpu.VMEM((mp, rows, width), BF),
                 pltpu.VMEM((mp, rows, width), BF),
                 pltpu.VMEM((rows, 2 * width), F32),
-                pltpu.VMEM((rows, width), BF),
-                pltpu.VMEM((rows, width), F32),
-                pltpu.VMEM((rows, width), F32),
-                pltpu.VMEM((rows, width), F32),
-                pltpu.VMEM((vn, width), F32),
-                pltpu.VMEM((vn, width), F32),
-                dma((12,)), dma((6,)),
+                dma((12,)),
                 dma((2,)), dma((2,)), dma((n,)), dma((n,)),
                 dma((mp,)), dma((mp,)), dma((mp,)), dma((mp,)),
                 dma((2,)), dma((2,)), dma((n,)), dma((n,)),

time: 20.7 us -> 20.3 us (0.981)
  Pallas kernels: 19.9 us -> 19.5 us
    pallas_call x1, Pallas kernels: 19 us -> 18.6 us  [step(): pl.pallas_call(functools.partial(kernel, n, mp, heads), out_shape=(jax.Sh...]
where the time goes in v4:
time: 20.3 us; the launch traced here: 20.1 us
  Pallas kernels  19.5 us (96%)
  between operations  0.64 us (3%)
    pallas_call x1, Pallas kernels, step(): pl.pallas_call(functools.partial(kernel, n, mp, heads), out_shape=(jax.Sh...  18.6 us
    pallas_call x1, Pallas kernels, step(): pl.pallas_call(hand_over, out_shape=tuple((jax.ShapeDtypeStruct(x.shape,...  0.82 us

profile of v4, /device:TPU:0, one launch (start us, length us, event | category | flops | bytes accessed | tf_op | source)
XLA Modules:
  0.0 20.1 jit_solution(10432305217009750736)
XLA Ops:
  0.6 18.6 %shard_map.163 = (bf16[256,128]{1,0:T(8,128)(2,1)S(1)}, f32[256,128]{1,0:T(8,128)S(1)}, f32[256,128]{1,0:T(8,128)S(1)}, f32[256,128]{1,0:T(8,128)S(1)}, f32[8,128]{1,0:T(8,128)S(1)}, /*index=5*/f32[8,128]{1,0:T(8,128)S(1)}) custom-call(s32[1,2]{1,0:T(1,128)} %live_hbm.1, s32[1,2,8]{2,1,0:T(2,128)} %bitcast.1, s32[2,4]{1,0:T(2,128)} %lmask_hbm.1, ...), custom_call_target="tpu_custom_call" | custom-call | flops 209715200 | bytes 2097152 | tf_op jit(solution)/shard_map/pallas_call | solution.py:387
  19.3 0.8 %shard_map.164 = (bf16[256,128]{1,0:T(8,128)(2,1)}, f32[256,128]{1,0:T(8,128)}, f32[256,128]{1,0:T(8,128)}, f32[256,128]{1,0:T(8,128)}, f32[8,128]{1,0:T(8,128)}, /*index=5*/f32[8,128]{1,0:T(8,128)}) custom-call(bf16[256,128]{1,0:T(8,128)(2,1)S(1)} %get-tuple-element.12.refs_0_, f32[256,128]{1,0:T(8,128)S(1)} %get-tuple-element.13.refs_1_, ...), custom_call_target="tpu_custom_call" | custom-call | bytes 1048576 | tf_op jit(solution)/shard_map/pallas_call | solution.py:433

commit v5 on v4

--- a/solution.py
+++ b/solution.py
@@ -140,7 +140,11 @@
     for c in halo:
         c.start()
 
-    for c in loads[3:6]:
+    loads[5].wait()
+    for d in range(1, mp):
+        cot_copy(d, mm_i).start()
+
+    for c in loads[3:5]:
         c.wait()
     virt = jnp.concatenate([vk_v[...].astype(F32), vv_v[...].astype(F32)], axis=1)
     virt = jnp.concatenate([virt, jnp.zeros((blk - vn, 2 * width), F32)], axis=0)
@@ -148,8 +152,6 @@
     taken = taken.astype(BF)
     mix_send[...] = taken.reshape(n * blk, 2 * width)
     each(n - 1, lambda d: mix_copy(d + 1).start())
-    for d in range(1, mp):
-        cot_copy(d, mm_i).start()
     kv[mix0 : mix0 + blk, :] = taken[0]
     for c in small[1:]:
         c.wait()
@@ -234,6 +236,13 @@
     each(n - 1, lambda d: mix_copy(d + 1).wait_recv())
     for c in chunks[2:]:
         stats.append(score(c))
+
+    loads[7].wait()
+    for d in range(1, mp):
+        cot_copy(d, lax.rem(mm_i + mp - d, mp)).wait_recv()
+    g_t = mm(w_v[...], jnp.concatenate([cot[i] for i in range(mp)], axis=1), NT)
+    g_t = g_t.astype(BF).astype(F32)
+    g_blocks = blocks(g_t)
 
     top = functools.reduce(jnp.maximum, [t for t, _ in stats])
     factor = [jnp.exp(t - top) for t, _ in stats]
@@ -255,7 +264,6 @@
         axis=0,
     )
     attn_t = attn_t.astype(BF).astype(F32)
-    loads[7].wait()
     attn = jnp.transpose(attn_t).astype(BF)
 
     def proj_copy(d):
@@ -271,11 +279,6 @@
     for d in range(1, mp):
         proj_copy(d).start()
 
-    for d in range(1, mp):
-        cot_copy(d, lax.rem(mm_i + mp - d, mp)).wait_recv()
-    g_t = mm(w_v[...], jnp.concatenate([cot[i] for i in range(mp)], axis=1), NT)
-    g_t = g_t.astype(BF).astype(F32)
-    g_blocks = blocks(g_t)
     prod = g_t * attn_t
     delta = jnp.concatenate(
         [jnp.sum(prod[h * hd : (h + 1) * hd, :], axis=0, keepdims=True) for h in range(heads)],

time: 20.3 us -> 20.1 us (level)
  no operation moved by 1% of the time
where the time goes in v5:
time: 20.1 us; the launch traced here: 19.9 us
  Pallas kernels  19.3 us (96%)
  between operations  0.64 us (3%)
    pallas_call x1, Pallas kernels, step(): pl.pallas_call(functools.partial(kernel, n, mp, heads), out_shape=(jax.Sh...  18.5 us
    pallas_call x1, Pallas kernels, step(): pl.pallas_call(hand_over, out_shape=tuple((jax.ShapeDtypeStruct(x.shape,...  0.82 us

profile of v5, /device:TPU:0, one launch (start us, length us, event | category | flops | bytes accessed | tf_op | source)
XLA Modules:
  0.0 19.9 jit_solution(12688066713272523307)
XLA Ops:
  0.6 18.5 %shard_map.163 = (bf16[256,128]{1,0:T(8,128)(2,1)S(1)}, f32[256,128]{1,0:T(8,128)S(1)}, f32[256,128]{1,0:T(8,128)S(1)}, f32[256,128]{1,0:T(8,128)S(1)}, f32[8,128]{1,0:T(8,128)S(1)}, /*index=5*/f32[8,128]{1,0:T(8,128)S(1)}) custom-call(s32[1,2]{1,0:T(1,128)} %live_hbm.1, s32[1,2,8]{2,1,0:T(2,128)} %bitcast.1, s32[2,4]{1,0:T(2,128)} %lmask_hbm.1, ...), custom_call_target="tpu_custom_call" | custom-call | flops 209715200 | bytes 2097152 | tf_op jit(solution)/shard_map/pallas_call | solution.py:390
  19.1 0.8 %shard_map.164 = (bf16[256,128]{1,0:T(8,128)(2,1)}, f32[256,128]{1,0:T(8,128)}, f32[256,128]{1,0:T(8,128)}, f32[256,128]{1,0:T(8,128)}, f32[8,128]{1,0:T(8,128)}, /*index=5*/f32[8,128]{1,0:T(8,128)}) custom-call(bf16[256,128]{1,0:T(8,128)(2,1)S(1)} %get-tuple-element.12.refs_0_, f32[256,128]{1,0:T(8,128)S(1)} %get-tuple-element.13.refs_1_, ...), custom_call_target="tpu_custom_call" | custom-call | bytes 1048576 | tf_op jit(solution)/shard_map/pallas_call | solution.py:436

commit v6 on v5

--- a/solution.py
+++ b/solution.py
@@ -114,36 +114,6 @@
     picks = jnp.where(iota((2 * cap, rows), 1) == wanted, 1.0, 0.0).astype(BF)
     halo_send[...] = mm(picks, own, NN).astype(BF).reshape(2, cap, 2 * width)
 
-    pl.semaphore_wait(barrier, n - 1 + mp - 1)
-
-    def halo_copy(side):
-        start = rows + side * cap
-        return pltpu.make_async_remote_copy(
-            halo_send.at[side], kv.at[start : start + cap, :], halo_s.at[side], halo_r.at[side],
-            device_id={"nodes": right if side == 0 else left}, device_id_type=MESH,
-        )
-
-    def mix_copy(d):
-        return pltpu.make_async_remote_copy(
-            mix_send.at[pl.ds(d * blk, blk), :], kv.at[pl.ds(mix0 + d * blk, blk), :],
-            mix_s.at[d], mix_r.at[d],
-            device_id={"nodes": lax.rem(me + d, n)}, device_id_type=MESH,
-        )
-
-    def cot_copy(d, slot):
-        return pltpu.make_async_remote_copy(
-            cot.at[slot], cot.at[slot], cot_s.at[d], cot_r.at[d],
-            device_id={"mp": lax.rem(mm_i + d, mp)}, device_id_type=MESH,
-        )
-
-    halo = [halo_copy(0), halo_copy(1)]
-    for c in halo:
-        c.start()
-
-    loads[5].wait()
-    for d in range(1, mp):
-        cot_copy(d, mm_i).start()
-
     for c in loads[3:5]:
         c.wait()
     virt = jnp.concatenate([vk_v[...].astype(F32), vv_v[...].astype(F32)], axis=1)
@@ -151,7 +121,38 @@
     taken = mm(onehot[...], own, NN).reshape(n, blk, 2 * width) + virt[None]
     taken = taken.astype(BF)
     mix_send[...] = taken.reshape(n * blk, 2 * width)
+
+    pl.semaphore_wait(barrier, n - 1 + mp - 1)
+
+    def halo_copy(side):
+        start = rows + side * cap
+        return pltpu.make_async_remote_copy(
+            halo_send.at[side], kv.at[start : start + cap, :], halo_s.at[side], halo_r.at[side],
+            device_id={"nodes": right if side == 0 else left}, device_id_type=MESH,
+        )
+
+    def mix_copy(d):
+        return pltpu.make_async_remote_copy(
+            mix_send.at[pl.ds(d * blk, blk), :], kv.at[pl.ds(mix0 + d * blk, blk), :],
+            mix_s.at[d], mix_r.at[d],
+            device_id={"nodes": lax.rem(me + d, n)}, device_id_type=MESH,
+        )
+
+    def cot_copy(d, slot):
+        return pltpu.make_async_remote_copy(
+            cot.at[slot], cot.at[slot], cot_s.at[d], cot_r.at[d],
+            device_id={"mp": lax.rem(mm_i + d, mp)}, device_id_type=MESH,
+        )
+
     each(n - 1, lambda d: mix_copy(d + 1).start())
+    halo = [halo_copy(0), halo_copy(1)]
+    for c in halo:
+        c.start()
+
+    loads[5].wait()
+    for d in range(1, mp):
+        cot_copy(d, mm_i).start()
+
     kv[mix0 : mix0 + blk, :] = taken[0]
     for c in small[1:]:
         c.wait()

time: 20.1 us -> 20.4 us (1.015)
  Pallas kernels: 19.3 us -> 19.6 us
    pallas_call x1, Pallas kernels: 18.5 us -> 18.8 us  [step(): pl.pallas_call(functools.partial(kernel, n, mp, heads), out_shape=(jax.Sh...]
where the time goes in v6:
time: 20.4 us; the launch traced here: 20.3 us
  Pallas kernels  19.6 us (96%)
  between operations  0.64 us (3%)
    pallas_call x1, Pallas kernels, step(): pl.pallas_call(functools.partial(kernel, n, mp, heads), out_shape=(jax.Sh...  18.8 us
    pallas_call x1, Pallas kernels, step(): pl.pallas_call(hand_over, out_shape=tuple((jax.ShapeDtypeStruct(x.shape,...  0.82 us

profile of v6, /device:TPU:0, one launch (start us, length us, event | category | flops | bytes accessed | tf_op | source)
XLA Modules:
  0.0 20.3 jit_solution(14177564440846518670)
XLA Ops:
  0.6 18.8 %shard_map.163 = (bf16[256,128]{1,0:T(8,128)(2,1)S(1)}, f32[256,128]{1,0:T(8,128)S(1)}, f32[256,128]{1,0:T(8,128)S(1)}, f32[256,128]{1,0:T(8,128)S(1)}, f32[8,128]{1,0:T(8,128)S(1)}, /*index=5*/f32[8,128]{1,0:T(8,128)S(1)}) custom-call(s32[1,2]{1,0:T(1,128)} %live_hbm.1, s32[1,2,8]{2,1,0:T(2,128)} %bitcast.1, s32[2,4]{1,0:T(2,128)} %lmask_hbm.1, ...), custom_call_target="tpu_custom_call" | custom-call | flops 209715200 | bytes 2097152 | tf_op jit(solution)/shard_map/pallas_call | solution.py:391
  19.5 0.8 %shard_map.164 = (bf16[256,128]{1,0:T(8,128)(2,1)}, f32[256,128]{1,0:T(8,128)}, f32[256,128]{1,0:T(8,128)}, f32[256,128]{1,0:T(8,128)}, f32[8,128]{1,0:T(8,128)}, /*index=5*/f32[8,128]{1,0:T(8,128)}) custom-call(bf16[256,128]{1,0:T(8,128)(2,1)S(1)} %get-tuple-element.12.refs_0_, f32[256,128]{1,0:T(8,128)S(1)} %get-tuple-element.13.refs_1_, ...), custom_call_target="tpu_custom_call" | custom-call | bytes 1048576 | tf_op jit(solution)/shard_map/pallas_call | solution.py:437
